TPU v7x, 32 devices: a whole 2x2x4 slice. The times are simulated.
32 devices in a mesh: segment: 4 (over y, core), chan: 4 (over z), tm: 2 (over x).
Axes of the slice: x: 2, y: 2, z: 4, core: 2. Of those that a mesh axis runs over, the one named last changes fastest.
Arguments:
- voltages: bfloat16 [3, 512, 2048, 128], P(None, 'chan', ('segment', 'tm')), may hold values from -6 to 6
- flags: int32 [512], P('chan'), may hold values 0 or 1
- delays: int32 [512, 512], replicated, may hold values from 0 to 127
- analysis_taps: float32 [4, 64], replicated, may hold values from -3 to 3
- synthesis_taps: float32 [4, 64], replicated, may hold values from -3 to 3
Outputs:
- vis: float32 [64, 8, 2, 512, 512], P('chan', ('segment', 'tm'))
- beams: bfloat16 [3, 512, 2048, 128], P(None, 'chan', ('segment', 'tm'))
All inputs are finite; a program needn't handle non-finite values. No bound on the sum of `flags` on one device may be relied on, other than what follows from the above.
Results may differ from a plain program's by a relative error of at most 0.008.
Values may be sent and summed in bfloat16 or wider, within the bound.
A program may use at most 256 MiB of HBM per device.

v0:
```python
import math
import jax
import jax.numpy as jnp
from jax import lax
from jax.sharding import PartitionSpec as P

A = 512
C = 64
TAPS = 4
FB = 256
MB = 3


def shifted(value, axis, steps):
    count = lax.axis_size(axis)
    leading, last = (max(0, -steps), min(count, count - steps))
    return lax.ppermute(value, axis, [(source, source + steps) for source in range(leading, last)])


def forward_table(chan_count):
    indices = jnp.arange(2 * chan_count, dtype=jnp.int32)
    out_chan = indices // 2
    out_part = indices % 2
    in_part = indices // chan_count
    in_sample = indices % chan_count
    wrapped = out_chan[:, None] * in_sample[None, :] % chan_count
    angles = wrapped.astype(jnp.float32) * (2.0 * math.pi / chan_count)
    cosine = jnp.cos(angles)
    sine_part = jnp.sin(angles)
    real_row = jnp.where(in_part[None, :] == 0, cosine, sine_part)
    imag_row = jnp.where(in_part[None, :] == 0, -sine_part, cosine)
    dft_table = jnp.where(out_part[:, None] == 0, real_row, imag_row)
    return (dft_table * (1.0 / math.sqrt(chan_count))).astype(jnp.bfloat16)


def inverse_table(chan_count):
    indices = jnp.arange(2 * chan_count, dtype=jnp.int32)
    out_part = indices // chan_count
    out_sample = indices % chan_count
    in_chan = indices // 2
    in_part = indices % 2
    wrapped = out_sample[:, None] * in_chan[None, :] % chan_count
    angles = wrapped.astype(jnp.float32) * (2.0 * math.pi / chan_count)
    cosine = jnp.cos(angles)
    sine_part = jnp.sin(angles)
    real_row = jnp.where(in_part[None, :] == 0, cosine, -sine_part)
    imag_row = jnp.where(in_part[None, :] == 0, sine_part, cosine)
    dft_table = jnp.where(out_part[:, None] == 0, real_row, imag_row)
    return (dft_table * (1.0 / math.sqrt(chan_count))).astype(jnp.bfloat16)


def steering_weights(delays, channel_list, chan_count):
    odd_steps = 2 * channel_list + 1
    wrapped = odd_steps[:, None, None] * delays[None, :, :] % (2 * chan_count)
    angles = wrapped.astype(jnp.float32) * (math.pi / chan_count)
    cosine = jnp.swapaxes(jnp.cos(angles), 1, 2)
    sine_part = jnp.swapaxes(jnp.sin(angles), 1, 2)
    upper = jnp.concatenate([cosine, sine_part], axis=2)
    lower = jnp.concatenate([-sine_part, cosine], axis=2)
    return jnp.concatenate([upper, lower], axis=1).astype(jnp.bfloat16)


def channelize(block, rim, paired_filter_taps, forward, flag_scale):
    history = paired_filter_taps.shape[0] - 1
    frames = block.shape[1]
    padded = jnp.concatenate([rim.astype(jnp.float32), block.astype(jnp.float32)], axis=1)
    weighted = paired_filter_taps[0] * padded[:, history : history + frames]
    for tap_number in range(1, history + 1):
        weighted = (
            weighted
            + paired_filter_taps[tap_number]
            * padded[:, history - tap_number : history - tap_number + frames]
        )
    weighted = weighted.astype(jnp.bfloat16)
    spectra = jnp.einsum("oi,afi->oaf", forward, weighted, preferred_element_type=jnp.float32)
    spectra = spectra * flag_scale[None, :, None]
    return spectra.astype(jnp.bfloat16).reshape(forward.shape[0] // 2, 2, block.shape[0], frames)


def gram_block(turned):
    left_part = jnp.concatenate([turned[:, 0], turned[:, 1]], axis=-1)
    rotated = jnp.concatenate([turned[:, 1], -turned[:, 0]], axis=-1)
    stacked = jnp.concatenate([left_part, rotated], axis=1)
    return jnp.einsum("cif,cjf->cij", stacked, left_part, preferred_element_type=jnp.float32)


def form_beams(turned, steering_matrix):
    chan_local, parts, antennas, frames = turned.shape
    flattened_rows = turned.reshape(chan_local, parts * antennas, frames)
    formed_beams = jnp.einsum(
        "goq,gqk->gok", steering_matrix, flattened_rows, preferred_element_type=jnp.float32
    )
    formed_beams = (formed_beams * (1.0 / math.sqrt(antennas))).astype(jnp.bfloat16)
    return formed_beams.reshape(chan_local, 2, steering_matrix.shape[1] // 2, frames)


def tail_frames(inverse_part, count, history):
    beam_local, frames, width_both = inverse_part.shape
    block_frames = frames // count
    blocks = inverse_part.reshape(beam_local, count, block_frames, width_both)
    return blocks[:, :, block_frames - history :, :]


def synthesize(inverse_part, tails, count, paired_filter_taps):
    history = paired_filter_taps.shape[0] - 1
    beam_local, frames, width_both = inverse_part.shape
    block_frames = frames // count
    blocks = inverse_part.reshape(beam_local, count, block_frames, width_both)
    padded = jnp.concatenate([tails.astype(jnp.float32), blocks.astype(jnp.float32)], axis=2)
    weighted = paired_filter_taps[0] * padded[:, :, history : history + block_frames]
    for tap_number in range(1, history + 1):
        weighted = (
            weighted
            + paired_filter_taps[tap_number]
            * padded[:, :, history - tap_number : history - tap_number + block_frames]
        )
    return jnp.transpose(weighted.astype(jnp.bfloat16), (1, 0, 2, 3))


def per_device(voltages, flags, delays, analysis_taps, synthesis_taps):
    chan_local = C // lax.axis_size("chan")
    history = TAPS - 1
    forward = forward_table(C)
    inverse_result = inverse_table(C)
    analysis_both = jnp.concatenate([analysis_taps, analysis_taps], axis=1)
    synthesis_both = jnp.concatenate([synthesis_taps, synthesis_taps], axis=1)
    flag_scale = flags.astype(jnp.float32)
    channel_list = lax.axis_index("chan") * chan_local + jnp.arange(chan_local, dtype=jnp.int32)
    steering_matrix = steering_weights(delays, channel_list, C)
    rims_all = shifted(voltages[:, :, FB - history :, :], ("segment", "tm"), 1)
    rim_list = [rims_all[batch_step] for batch_step in range(MB)]
    spectra_list = [
        channelize(voltages[batch_step], rim_list[batch_step], analysis_both, forward, flag_scale)
        for batch_step in range(MB)
    ]
    gram_total = None
    beam_list = []
    for batch_step in range(MB):
        turned = lax.all_to_all(
            spectra_list[batch_step], "chan", split_axis=0, concat_axis=2, tiled=True
        )
        gram_piece = gram_block(turned)
        gram_total = gram_piece if batch_step == 0 else gram_total + gram_piece
        piece = lax.all_to_all(
            form_beams(turned, steering_matrix), "chan", split_axis=2, concat_axis=0, tiled=True
        )
        chan_all, parts, beam_local, frames = piece.shape
        flattened_rows = piece.reshape(chan_all * parts, beam_local, frames)
        result = jnp.einsum(
            "oi,ibf->bfo", inverse_result, flattened_rows, preferred_element_type=jnp.float32
        )
        inverse_single = result.astype(jnp.bfloat16)
        tails = shifted(tail_frames(inverse_single, 1, history), ("segment", "tm"), 1)
        beam_list.append(synthesize(inverse_single, tails, 1, synthesis_both))
    beams = jnp.concatenate(beam_list, axis=0)
    vis = (gram_total * (1.0 / (MB * FB))).reshape(chan_local, 1, 2, A, A)
    return (vis, beams)


def solution(mesh):
    placed = (P(None, "chan", ("segment", "tm"), None), P("chan"), P(), P(), P())
    return jax.shard_map(
        per_device,
        mesh=mesh,
        in_specs=placed,
        out_specs=(
            P("chan", ("segment", "tm"), None, None, None),
            P(None, "chan", ("segment", "tm"), None),
        ),
        check_vma=False,
    )
```

profile of v0, /device:TPU:0, one launch (start us, length us, event | category | flops | bytes accessed | tf_op | source)
XLA Modules:
  0.0 1388.2 jit_solution(14261170279806623218)
XLA Ops:
  0.6 1.3 slice.151
  2.0 4.9 collective-permute-start
  7.0 23.4 %bitcast_convert_fusion = (f32[128,256,128]{2,1,0:T(8,128)}, f32[128,256,128]{2,1,0:T(8,128)}, f32[128,256,128]{2,1,0:T(8,128)}) fusion(bf16[3,128,256,128]{3,2,1,0:T(8,128)(2,1)} %param.5), kind=kLoop, calls=%fused_computation.133 | loop fusion | flops 12582912 | bytes 75497472 | tf_op jit(solution)/shard_map/convert_element_type | solution.py:66
  30.7 32.0 %multiply_convert_fusion.3 = bf16[128,128,256]{2,0,1:T(8,128)(2,1)} fusion(f32[128]{0:T(128)S(1)} %convert_element_type.152, f32[128,3,128]{2,1,0:T(4,128)S(1)} %copy.50, f32[128,256,128]{2,1,0:T(8,128)} %get-tuple-element.10, f32[128]{0:T(128)S(1)} %get-tuple-element.33, f32[128]{0:T(128)S(1)} %get-tuple-element.34, f32[128]{0:T(128)S(1)} %get-tuple-element.35, ...), kind=kOutput, calls=%fused_computation.121 | convolution fusion | flops 1128595456 | bytes 25366272 | tf_op jit(solution)/shard_map/oi,afi->oaf/dot_general | solution.py:75
  62.7 13.1 reshape.197
  75.8 8.1 copy.51
  83.9 5.6 all-to-all-start.2
  89.7 32.3 %multiply_convert_fusion.4 = bf16[128,128,256]{2,0,1:T(8,128)(2,1)} fusion(f32[128]{0:T(128)S(1)} %convert_element_type.152, f32[128,3,128]{2,1,0:T(4,128)S(1)} %copy.47, f32[128,256,128]{2,1,0:T(8,128)} %get-tuple-element.12, f32[128]{0:T(128)S(1)} %get-tuple-element.33, f32[128]{0:T(128)S(1)} %get-tuple-element.34, f32[128]{0:T(128)S(1)} %get-tuple-element.35, ...), kind=kOutput, calls=%fused_computation.122 | convolution fusion | flops 1128595456 | bytes 25366272 | tf_op jit(solution)/shard_map/oi,afi->oaf/dot_general | solution.py:75
  122.0 13.1 reshape.196
  135.1 8.2 copy.48
  143.3 129.3 %all-to-all-done.2 = bf16[64,2,128,256]{3,1,2,0:T(2,128)(2,1)} async-done(((bf16[64,2,128,256]{3,1,2,0:T(2,128)(2,1)}), bf16[64,2,128,256]{3,1,2,0:T(2,128)(2,1)}, u32[]{:S(2)}, u32[]{:S(2)}) %all-to-all-start.2) | async-done | bytes 8388640 | tf_op jit(solution)/shard_map/all_to_all | solution.py:139
  272.6 5.8 all-to-all-start.1
  278.6 31.9 %multiply_convert_fusion.5 = bf16[128,128,256]{2,0,1:T(8,128)(2,1)} fusion(f32[128]{0:T(128)S(1)} %convert_element_type.152, f32[128,3,128]{2,1,0:T(4,128)S(1)} %copy.44, f32[128,256,128]{2,1,0:T(8,128)} %get-tuple-element.11, f32[128]{0:T(128)S(1)} %get-tuple-element.33, f32[128]{0:T(128)S(1)} %get-tuple-element.34, f32[128]{0:T(128)S(1)} %get-tuple-element.35, ...), kind=kOutput, calls=%fused_computation.123 | convolution fusion | flops 1128595456 | bytes 25366272 | tf_op jit(solution)/shard_map/oi,afi->oaf/dot_general | solution.py:75
  310.5 13.1 reshape.195
  323.5 8.2 copy.45
  331.7 129.2 %all-to-all-done.1 = bf16[64,2,128,256]{3,1,2,0:T(2,128)(2,1)} async-done(((bf16[64,2,128,256]{3,1,2,0:T(2,128)(2,1)}), bf16[64,2,128,256]{3,1,2,0:T(2,128)(2,1)}, u32[]{:S(2)}, u32[]{:S(2)}) %all-to-all-start.1) | async-done | bytes 8388640 | tf_op jit(solution)/shard_map/all_to_all | solution.py:139
  461.0 5.7 all-to-all-start
  467.0 70.0 %fusion.102 = (bf16[16,512,512]{2,1,0:T(8,128)(2,1)}, bf16[16,512,512]{2,1,0:T(8,128)(2,1)}, bf16[16,512,512]{2,1,0:T(8,128)(2,1)}) fusion(s32[512,512]{1,0:T(8,128)S(1)} %copy.53, s32[16]{0:T(128)S(1)} %multiply_add_fusion), kind=kLoop, calls=%fused_computation.143 | loop fusion | flops 75497472 | bytes 26214464 | tf_op jit(solution)/shard_map/convert.11
  537.0 8.5 copy.71
  545.5 21.3 %multiply_convert_fusion.1 = bf16[16,1024,256]{2,1,0:T(8,128)(2,1)} fusion(bf16[16,1024,256]{2,1,0:T(8,128)(2,1)} %bitcast.191, bf16[16,512,512]{2,1,0:T(8,128)(2,1)} %get-tuple-element.21, bf16[16,512,512]{2,1,0:T(8,128)(2,1)} %get-tuple-element.20, bf16[16,512,512]{2,1,0:T(8,128)(2,1)} %get-tuple-element.19), kind=kOutput, calls=%fused_computation.117 | convolution fusion | flops 8732540928 | bytes 41943040 | tf_op jit(solution)/shard_map/goq,gqk->gok/dot_general | solution.py:90
  566.8 16.5 %copy.60 = bf16[16,2,512,256]{3,1,0,2:T(2,128)(2,1)} copy(bf16[16,2,512,256]{3,2,1,0:T(8,128)(2,1)} %bitcast.192) | data formatting | bytes 16777216 | tf_op jit(solution)/shard_map/reshape | solution.py:94
  583.3 66.0 %all-to-all-done = bf16[64,2,128,256]{3,1,2,0:T(2,128)(2,1)} async-done(((bf16[64,2,128,256]{3,1,2,0:T(2,128)(2,1)}), bf16[64,2,128,256]{3,1,2,0:T(2,128)(2,1)}, u32[]{:S(2)}, u32[]{:S(2)}) %all-to-all-start) | async-done | bytes 8388640 | tf_op jit(solution)/shard_map/all_to_all | solution.py:139
  649.3 6.0 all-to-all-start.4
  655.3 8.5 copy.70
  663.8 21.3 %multiply_convert_fusion.2 = bf16[16,1024,256]{2,1,0:T(8,128)(2,1)} fusion(bf16[16,1024,256]{2,1,0:T(8,128)(2,1)} %bitcast.194, bf16[16,512,512]{2,1,0:T(8,128)(2,1)} %get-tuple-element.21, bf16[16,512,512]{2,1,0:T(8,128)(2,1)} %get-tuple-element.20, bf16[16,512,512]{2,1,0:T(8,128)(2,1)} %get-tuple-element.19), kind=kOutput, calls=%fused_computation.118 | convolution fusion | flops 8732540928 | bytes 41943040 | tf_op jit(solution)/shard_map/goq,gqk->gok/dot_general | solution.py:90
  685.1 16.4 %copy.55 = bf16[16,2,512,256]{3,1,0,2:T(2,128)(2,1)} copy(bf16[16,2,512,256]{3,2,1,0:T(8,128)(2,1)} %bitcast.193) | data formatting | bytes 16777216 | tf_op jit(solution)/shard_map/reshape | solution.py:94
  701.5 136.4 %all-to-all-done.4 = bf16[16,2,512,256]{3,1,0,2:T(2,128)(2,1)} async-done(((bf16[16,2,512,256]{3,1,0,2:T(2,128)(2,1)}), bf16[16,2,512,256]{3,1,0,2:T(2,128)(2,1)}, u32[]{:S(2)}, u32[]{:S(2)}) %all-to-all-start.4) | async-done | bytes 8388640 | tf_op jit(solution)/shard_map/all_to_all | solution.py:144
  838.0 5.6 all-to-all-start.3
  844.3 8.6 copy.49
  852.9 8.6 copy.46
  861.5 8.4 copy.72
  870.0 8.4 copy.52
  878.4 21.4 %multiply_convert_fusion = bf16[16,1024,256]{2,1,0:T(8,128)(2,1)} fusion(bf16[16,1024,256]{2,1,0:T(8,128)(2,1)} %bitcast.189, bf16[16,512,512]{2,1,0:T(8,128)(2,1)} %get-tuple-element.21, bf16[16,512,512]{2,1,0:T(8,128)(2,1)} %get-tuple-element.20, bf16[16,512,512]{2,1,0:T(8,128)(2,1)} %get-tuple-element.19), kind=kOutput, calls=%fused_computation.116 | convolution fusion | flops 8732540928 | bytes 41943040 | tf_op jit(solution)/shard_map/goq,gqk->gok/dot_general | solution.py:90
  899.8 16.6 %copy.65 = bf16[16,2,512,256]{3,1,0,2:T(2,128)(2,1)} copy(bf16[16,2,512,256]{3,2,1,0:T(8,128)(2,1)} %bitcast.190) | data formatting | bytes 16777216 | tf_op jit(solution)/shard_map/reshape | solution.py:94
  916.4 4.6 fusion.174
  921.0 2.3 fusion.173
  923.3 4.1 slice_bitcast_fusion.3
  927.4 4.0 slice_bitcast_fusion.5
  931.6 3.6 slice_bitcast_fusion.1
  935.2 91.0 %all-to-all-done.3 = bf16[16,2,512,256]{3,1,0,2:T(2,128)(2,1)} async-done(((bf16[16,2,512,256]{3,1,0,2:T(2,128)(2,1)}), bf16[16,2,512,256]{3,1,0,2:T(2,128)(2,1)}, u32[]{:S(2)}, u32[]{:S(2)}) %all-to-all-start.3) | async-done | bytes 8388640 | tf_op jit(solution)/shard_map/all_to_all | solution.py:144
  1026.3 5.8 all-to-all-start.5
  1032.1 4.4 fusion.175
  1036.5 23.4 %fusion.60 = f32[16,1024,512]{2,1,0:T(8,128)} fusion(bf16[16,512,256]{2,1,0:T(8,128)(2,1)} %fusion.173, bf16[16,512,256]{2,1,0:T(8,128)(2,1)} %get-tuple-element.18, bf16[16,512,256]{2,1,0:T(8,128)(2,1)} %get-tuple-element.17), kind=kOutput, calls=%fused_computation.92 | convolution fusion | flops 8673820672 | bytes 46137344 | tf_op jit(solution)/shard_map/cif,cjf->cij/dot_general | solution.py:84
  1059.9 22.4 %fusion.68 = f32[16,1024,512]{2,1,0:T(8,128)} fusion(bf16[16,512,256]{2,1,0:T(8,128)(2,1)S(1)} %copy-done.2, bf16[16,512,256]{2,1,0:T(8,128)(2,1)} %get-tuple-element.16, bf16[16,512,256]{2,1,0:T(8,128)(2,1)} %get-tuple-element.15), kind=kOutput, calls=%fused_computation.100 | convolution fusion | flops 8673820672 | bytes 46137344 | tf_op jit(solution)/shard_map/cif,cjf->cij/dot_general | solution.py:84
  1082.3 40.6 %add_multiply_fusion = f32[16,1024,512]{2,1,0:T(8,128)} fusion(f32[16,1024,512]{2,1,0:T(8,128)} %fusion.60, f32[16,1024,512]{2,1,0:T(8,128)} %fusion.68, bf16[16,512,256]{2,1,0:T(8,128)(2,1)} %fusion.175, bf16[16,512,256]{2,1,0:T(8,128)(2,1)} %get-tuple-element.14, bf16[16,512,256]{2,1,0:T(8,128)(2,1)} %get-tuple-element.13), kind=kOutput, calls=%fused_computation.1 | convolution fusion | flops 8698986496 | bytes 113246208 | tf_op jit(solution)/shard_map/cif,cjf->cij/dot_general | solution.py:84
  1123.0 11.6 copy.61
  1134.5 7.8 copy.62
  1142.3 19.6 %fusion.112 = bf16[128,256,128]{2,1,0:T(8,128)(2,1)S(1)} fusion(bf16[128,128,256]{2,1,0:T(8,128)(2,1)} %bitcast.185, s32[128]{0:T(128)S(1)} %copy-done.11, s32[128]{0:T(128)S(1)} %copy-done.9, pred[128]{0:T(512)(128)(4,1)S(1)} %copy-done.5, pred[128]{0:T(512)(128)(4,1)S(1)} %copy-done.7), kind=kOutput, calls=%fused_computation.148 | convolution fusion | flops 1078263808 | bytes 16778496 | tf_op jit(solution)/shard_map/oi,ibf->bfo/dot_general | solution.py:149
  1161.9 3.3 copy-done
  1165.3 4.8 collective-permute-start.2
  1170.1 11.6 copy.56
  1181.7 7.8 copy.57
  1189.4 19.4 %fusion.109 = bf16[128,256,128]{2,1,0:T(8,128)(2,1)S(1)} fusion(bf16[128,128,256]{2,1,0:T(8,128)(2,1)} %bitcast.187, s32[128]{0:T(128)S(1)} %copy-done.11, s32[128]{0:T(128)S(1)} %copy-done.9, pred[128]{0:T(512)(128)(4,1)S(1)} %copy-done.5, pred[128]{0:T(512)(128)(4,1)S(1)} %copy-done.7), kind=kOutput, calls=%fused_computation.147 | convolution fusion | flops 1078263808 | bytes 16778496 | tf_op jit(solution)/shard_map/oi,ibf->bfo/dot_general | solution.py:149
  1208.9 3.3 copy-done.1
  1212.2 2.3 collective-permute-start.1
  1214.6 11.8 convert_bitcast_fusion.2
  1226.4 11.5 copy.66
  1237.8 7.7 copy.67
  1245.6 22.7 %fusion.115 = bf16[128,256,128]{2,1,0:T(8,128)(2,1)} fusion(bf16[128,128,256]{2,1,0:T(8,128)(2,1)} %bitcast.183, s32[128]{0:T(128)S(1)} %copy-done.11, s32[128]{0:T(128)S(1)} %copy-done.9, pred[128]{0:T(512)(128)(4,1)S(1)} %copy-done.5, pred[128]{0:T(512)(128)(4,1)S(1)} %copy-done.7), kind=kOutput, calls=%fused_computation.149 | convolution fusion | flops 1078263808 | bytes 16778496 | tf_op jit(solution)/shard_map/oi,ibf->bfo/dot_general | solution.py:149
  1268.2 11.6 convert_bitcast_fusion
  1280.9 2.4 collective-permute-start.3
  1283.3 11.4 convert_bitcast_fusion.1
  1294.9 72.4 %fusion.108 = (bf16[1,128,256,128]{3,2,1,0:T(8,128)(2,1)}, bf16[1,128,256,128]{3,2,1,0:T(8,128)(2,1)}, bf16[1,128,256,128]{3,2,1,0:T(8,128)(2,1)}) fusion(f32[128,1,256,128]{3,2,0,1:T(8,128)} %convert_bitcast_fusion.2, f32[128,1,3,128]{3,2,0,1:T(4,128)S(1)} %convert_element_type.172, f32[128]{0:T(128)S(1)} %copy-done.15, f32[128]{0:T(128)S(1)} %copy-done.16, ...), kind=kLoop, calls=%fused_computation.146 | loop fusion | flops 150994944 | bytes 101255168 | tf_op jit(solution)/shard_map/transpose | solution.py:117
  1367.3 20.7 %pad_maximum_fusion = bf16[3,128,256,128]{3,2,1,0:T(8,128)(2,1)} fusion(bf16[1,128,256,128]{3,2,1,0:T(8,128)(2,1)} %get-tuple-element.27, bf16[1,128,256,128]{3,2,1,0:T(8,128)(2,1)} %get-tuple-element.26, bf16[1,128,256,128]{3,2,1,0:T(8,128)(2,1)} %get-tuple-element.25), kind=kLoop, calls=%fused_computation.5 | loop fusion | flops 25165824 | bytes 50331648 | tf_op jit(solution)/shard_map/concatenate | solution.py:155
  (76 shorter events, 3.2 us)
Async XLA Ops:
  2.0 28.5 %collective-permute-start = (bf16[3,128,3,128]{3,1,2,0:T(8,128)(2,1)S(1)}, bf16[3,128,3,128]{3,1,2,0:T(8,128)(2,1)S(1)}, u32[]{:S(2)}, u32[]{:S(2)}) collective-permute-start(bf16[3,128,3,128]{3,1,2,0:T(8,128)(2,1)S(1)} %copy.73), channel_id=1, source_target_pairs={{0,1},{1,8},{8,9},{9,16},{16,17},{17,24},{24,25},{2,3},{3,10},{10,... | collective-permute-start | bytes 884744 | tf_op jit(solution)/shard_map/ppermute | solution.py:17
  6.9 271.6 %copy-start.4 = (pred[128]{0:T(512)(128)(4,1)}, pred[128]{0:T(512)(128)(4,1)S(1)}, u32[]{:S(2)}) copy-start(pred[128]{0:T(512)(128)(4,1)S(1)} %get-tuple-element.38) | copy-start | bytes 388
  6.9 271.6 %copy-start.6 = (pred[128]{0:T(512)(128)(4,1)}, pred[128]{0:T(512)(128)(4,1)S(1)}, u32[]{:S(2)}) copy-start(pred[128]{0:T(512)(128)(4,1)S(1)} %get-tuple-element.39) | copy-start | bytes 388
  7.0 23.5 %copy-start.18 = (s32[128]{0:T(128)S(1)}, s32[128]{0:T(128)}, u32[]{:S(2)}) copy-start(s32[128]{0:T(128)} %param.6) | copy-start | bytes 1540
  7.0 23.4 %copy-start.12 = (f32[4,64]{1,0:T(4,128)S(1)}, f32[4,64]{1,0:T(4,128)}, u32[]{:S(2)}) copy-start(f32[4,64]{1,0:T(4,128)} %param.8) | copy-start | bytes 3076
  30.5 248.1 %copy-start.8 = (s32[128]{0:T(128)}, s32[128]{0:T(128)S(1)}, u32[]{:S(2)}) copy-start(s32[128]{0:T(128)S(1)} %get-tuple-element.36) | copy-start | bytes 1540
  30.5 248.1 %copy-start.10 = (s32[128]{0:T(128)}, s32[128]{0:T(128)S(1)}, u32[]{:S(2)}) copy-start(s32[128]{0:T(128)S(1)} %get-tuple-element.37) | copy-start | bytes 1540
  83.9 188.7 %all-to-all-start.2 = ((bf16[64,2,128,256]{3,1,2,0:T(2,128)(2,1)}), bf16[64,2,128,256]{3,1,2,0:T(2,128)(2,1)}, u32[]{:S(2)}, u32[]{:S(2)}) async-start(bf16[64,2,128,256]{3,1,2,0:T(2,128)(2,1)} %copy.51), calls=%async_computation.2 | async-start | bytes 16777216 | tf_op jit(solution)/shard_map/all_to_all | solution.py:139
  272.6 188.4 %all-to-all-start.1 = ((bf16[64,2,128,256]{3,1,2,0:T(2,128)(2,1)}), bf16[64,2,128,256]{3,1,2,0:T(2,128)(2,1)}, u32[]{:S(2)}, u32[]{:S(2)}) async-start(bf16[64,2,128,256]{3,1,2,0:T(2,128)(2,1)} %copy.48), calls=%async_computation.1 | async-start | bytes 16777216 | tf_op jit(solution)/shard_map/all_to_all | solution.py:139
  323.5 143.1 %copy-start.3 = (s32[512,512]{1,0:T(8,128)S(1)}, s32[512,512]{1,0:T(8,128)}, u32[]{:S(2)}) copy-start(s32[512,512]{1,0:T(8,128)} %param.7) | copy-start | bytes 3145732
  461.0 188.3 %all-to-all-start = ((bf16[64,2,128,256]{3,1,2,0:T(2,128)(2,1)}), bf16[64,2,128,256]{3,1,2,0:T(2,128)(2,1)}, u32[]{:S(2)}, u32[]{:S(2)}) async-start(bf16[64,2,128,256]{3,1,2,0:T(2,128)(2,1)} %copy.45), calls=%async_computation | async-start | bytes 16777216 | tf_op jit(solution)/shard_map/all_to_all | solution.py:139
  649.3 188.7 %all-to-all-start.4 = ((bf16[16,2,512,256]{3,1,0,2:T(2,128)(2,1)}), bf16[16,2,512,256]{3,1,0,2:T(2,128)(2,1)}, u32[]{:S(2)}, u32[]{:S(2)}) async-start(bf16[16,2,512,256]{3,1,0,2:T(2,128)(2,1)} %copy.60), calls=%async_computation.4 | async-start | bytes 16777216 | tf_op jit(solution)/shard_map/all_to_all | solution.py:144
  685.1 158.5 %copy-start.13 = (f32[4,64]{1,0:T(4,128)S(1)}, f32[4,64]{1,0:T(4,128)}, u32[]{:S(2)}) copy-start(f32[4,64]{1,0:T(4,128)} %param.9) | copy-start | bytes 3076
  838.0 188.3 %all-to-all-start.3 = ((bf16[16,2,512,256]{3,1,0,2:T(2,128)(2,1)}), bf16[16,2,512,256]{3,1,0,2:T(2,128)(2,1)}, u32[]{:S(2)}, u32[]{:S(2)}) async-start(bf16[16,2,512,256]{3,1,0,2:T(2,128)(2,1)} %copy.55), calls=%async_computation.3 | async-start | bytes 16777216 | tf_op jit(solution)/shard_map/all_to_all | solution.py:144
  899.8 21.3 %slice-start.2 = ((s8[8388608]{0:T(1024)(128)(4,1)}), s8[4194304]{0:T(1024)(128)(4,1)S(1)}, s32[]{:S(2)}) async-start(s8[8388608]{0:T(1024)(128)(4,1)} %bitcast.175), calls=%async_computation.8 | async-start | bytes 8388608
  899.8 21.3 %slice-start.3 = ((s8[8388608]{0:T(1024)(128)(4,1)}), s8[4194304]{0:T(1024)(128)(4,1)S(1)}, s32[]{:S(2)}) async-start(s8[8388608]{0:T(1024)(128)(4,1)} %bitcast.175), calls=%async_computation.9 | async-start | bytes 8388608
  899.8 23.5 %slice-start.4 = ((s8[8388608]{0:T(1024)(128)(4,1)}), s8[4194304]{0:T(1024)(128)(4,1)S(1)}, s32[]{:S(2)}) async-start(s8[8388608]{0:T(1024)(128)(4,1)} %bitcast.180), calls=%async_computation.10 | async-start | bytes 8388608
  916.4 6.9 slice-start.5
  923.3 8.1 slice-start
  927.4 4.2 slice-start.1
  1026.3 200.1 %all-to-all-start.5 = ((bf16[16,2,512,256]{3,1,0,2:T(2,128)(2,1)}), bf16[16,2,512,256]{3,1,0,2:T(2,128)(2,1)}, u32[]{:S(2)}, u32[]{:S(2)}) async-start(bf16[16,2,512,256]{3,1,0,2:T(2,128)(2,1)} %copy.65), calls=%async_computation.5 | async-start | bytes 16777216 | tf_op jit(solution)/shard_map/all_to_all | solution.py:144
  1036.5 23.4 %copy-start.2 = (bf16[16,512,256]{2,1,0:T(8,128)(2,1)S(1)}, bf16[16,512,256]{2,1,0:T(8,128)(2,1)}, u32[]{:S(2)}) copy-start(bf16[16,512,256]{2,1,0:T(8,128)(2,1)} %fusion.174) | copy-start | bytes 12582916
  1122.9 19.4 %copy-start.5 = (pred[128]{0:T(512)(128)(4,1)S(1)}, pred[128]{0:T(512)(128)(4,1)}, u32[]{:S(2)}) copy-start(pred[128]{0:T(512)(128)(4,1)} %copy-done.4) | copy-start | bytes 388
  1122.9 19.4 %copy-start.7 = (pred[128]{0:T(512)(128)(4,1)S(1)}, pred[128]{0:T(512)(128)(4,1)}, u32[]{:S(2)}) copy-start(pred[128]{0:T(512)(128)(4,1)} %copy-done.6) | copy-start | bytes 388
  1123.0 19.4 %copy-start.9 = (s32[128]{0:T(128)S(1)}, s32[128]{0:T(128)}, u32[]{:S(2)}) copy-start(s32[128]{0:T(128)} %copy-done.8) | copy-start | bytes 1540
  1123.0 19.4 %copy-start.11 = (s32[128]{0:T(128)S(1)}, s32[128]{0:T(128)}, u32[]{:S(2)}) copy-start(s32[128]{0:T(128)} %copy-done.10) | copy-start | bytes 1540
  1161.9 3.3 copy-start
  1165.3 129.4 %collective-permute-start.2 = (bf16[128,1,3,128]{3,2,0,1:T(4,128)(2,1)S(1)}, bf16[128,1,3,128]{3,2,0,1:T(4,128)(2,1)S(1)}, u32[]{:S(2)}, u32[]{:S(2)}) collective-permute-start(bf16[128,1,3,128]{3,2,0,1:T(4,128)(2,1)S(1)} %slice.216), channel_id=1, source_target_pairs={{0,1},{1,8},{8,9},{9,16},{16,17},{17,24},{24,25},{2,3},{3,10},{10,... | collective-permute-start | bytes 294920 | tf_op jit(solution)/shard_map/ppermute | solution.py:17
  1208.8 3.3 copy-start.1
  1212.2 82.5 %collective-permute-start.1 = (bf16[128,1,3,128]{3,2,0,1:T(4,128)(2,1)S(1)}, bf16[128,1,3,128]{3,2,0,1:T(4,128)(2,1)S(1)}, u32[]{:S(2)}, u32[]{:S(2)}) collective-permute-start(bf16[128,1,3,128]{3,2,0,1:T(4,128)(2,1)S(1)} %slice.211), channel_id=1, source_target_pairs={{0,1},{1,8},{8,9},{9,16},{16,17},{17,24},{24,25},{2,3},{3,10},{10,... | collective-permute-start | bytes 294920 | tf_op jit(solution)/shard_map/ppermute | solution.py:17
  1279.9 15.0 %copy-start.14 = (f32[128]{0:T(128)S(1)}, f32[128]{0:T(128)}, u32[]{:S(2)}) copy-start(f32[128]{0:T(128)} %get-tuple-element.28) | copy-start | bytes 1540
  1279.9 15.0 %copy-start.15 = (f32[128]{0:T(128)S(1)}, f32[128]{0:T(128)}, u32[]{:S(2)}) copy-start(f32[128]{0:T(128)} %get-tuple-element.29) | copy-start | bytes 1540
  1279.9 15.0 %copy-start.16 = (f32[128]{0:T(128)S(1)}, f32[128]{0:T(128)}, u32[]{:S(2)}) copy-start(f32[128]{0:T(128)} %get-tuple-element.30) | copy-start | bytes 1540
  1279.9 15.0 %copy-start.17 = (f32[128]{0:T(128)S(1)}, f32[128]{0:T(128)}, u32[]{:S(2)}) copy-start(f32[128]{0:T(128)} %get-tuple-element.31) | copy-start | bytes 1540
  1280.9 13.9 collective-permute-start.3
where the time goes:
time: 1400 us; the launch traced here: 1390 us
  waiting for transfers between devices  552 us (39%)
  matrix products  308 us (22%)
  local copies, waits for them, and re-layouts  245 us (18%)
  other arithmetic  233 us (17%)
  starting transfers between devices  49 us (4%)
    all_to_all x3, waiting for transfers between devices, per_device(): lax.all_to_all(spectra_list[batch_step], 'chan', split_axis=0, concat_axi...  325 us
    all_to_all x3, waiting for transfers between devices, per_device(): lax.all_to_all(form_beams(turned, steering_matrix), 'chan', split_axis=2,...  227 us
    dot_general x3, matrix products, channelize(): jnp.einsum('oi,afi->oaf', forward, weighted, preferred_element_type=jnp.f...  96.2 us
    dot_general x3, matrix products, gram_block(): jnp.einsum('cif,cjf->cij', stacked, left_part, preferred_element_type=jnp...  86.4 us
    transpose x1, other arithmetic, synthesize(): return jnp.transpose(weighted.astype(jnp.bfloat16), (1, 0, 2, 3))  72.4 us
    another operation x1, other arithmetic  70 us
    dot_general x3, matrix products, form_beams(): jnp.einsum('goq,gqk->gok', steering_matrix, flattened_rows, preferred_ele...  63.9 us
    reshape x6, local copies, waits for them, and re-layouts, channelize(): spectra.astype(jnp.bfloat16)  63.7 us
  transfers between devices with their start and end apart: 10, of which 5 were waited for; matrix products, arithmetic and copies ran while one was open for 45% of the time, Pallas kernels for 0%

commit v1 on v0

--- a/solution.py
+++ b/solution.py
@@ -136,9 +136,21 @@
     gram_total = None
     beam_list = []
     for batch_step in range(MB):
-        turned = lax.all_to_all(
-            spectra_list[batch_step], "chan", split_axis=0, concat_axis=2, tiled=True
-        )
+        ways, here = (lax.axis_size("chan"), lax.axis_index("chan"))
+        width = spectra_list[batch_step].shape[0] // ways
+        lengths = list(spectra_list[batch_step].shape)
+        lengths[0] = width
+        height = lengths[2]
+        lengths[2] = height * ways
+        full = jnp.zeros(lengths, spectra_list[batch_step].dtype)
+        for mask in range(ways):
+            part = lax.dynamic_slice_in_dim(
+                spectra_list[batch_step], (here ^ mask) * width, width, axis=0
+            )
+            if mask:
+                part = lax.ppermute(part, "chan", [(d, d ^ mask) for d in range(ways)])
+            full = lax.dynamic_update_slice_in_dim(full, part, (here ^ mask) * height, axis=2)
+        turned = full
         gram_piece = gram_block(turned)
         gram_total = gram_piece if batch_step == 0 else gram_total + gram_piece
         piece = lax.all_to_all(

time: 1400 us -> 1550 us (1.11)
  starting transfers between devices: 49 us -> 168 us
  local copies, waits for them, and re-layouts: 245 us -> 279 us
    ppermute x0 -> x9, waiting for transfers between devices: none -> 546 us  [per_device(): part = lax.ppermute(part, 'chan', [(d, d ^ mask) for d in range(ways)])]
    all_to_all x3 -> x0, waiting for transfers between devices: 325 us -> none  [per_device(): lax.all_to_all(spectra_list[batch_step], 'chan', split_axis=0, concat_axi...]
    all_to_all x3, waiting for transfers between devices: 227 us -> 0.01 us  [per_device(): lax.all_to_all(form_beams(turned, steering_matrix), 'chan', split_axis=2,...]
    all_to_all x3, starting transfers between devices: 17.5 us -> 137 us  [per_device(): lax.all_to_all(form_beams(turned, steering_matrix), 'chan', split_axis=2,...]
    all_to_all x6 -> x0, local copies, waits for them, and re-layouts: 51.1 us -> none  [per_device(): lax.all_to_all(spectra_list[batch_step], 'chan', split_axis=0, concat_axi...]
    dynamic_update_slice x0 -> x15, local copies, waits for them, and re-layouts: none -> 48.3 us  [per_device(): lax.dynamic_update_slice_in_dim(full, part, (here ^ mask) * height, axis=2)]
    dynamic_slice x0 -> x3, local copies, waits for them, and re-layouts: none -> 28.3 us  [per_device(): lax.dynamic_slice_in_dim(spectra_list[batch_step], (here ^ mask) * width,...]
    reshape x6 -> x3, local copies, waits for them, and re-layouts: 63.7 us -> 39.3 us  [channelize(): spectra.astype(jnp.bfloat16)]
  transfers between devices with their start and end apart: 10 -> 16, of which waited for: 5 -> 6; matrix products, arithmetic and copies ran while one was open for 45% -> 40% of each run, Pallas kernels for 0% -> 0%
where the time goes in v1:
time: 1550 us; the launch traced here: 1540 us
  waiting for transfers between devices  546 us (35%)
  matrix products  309 us (20%)
  local copies, waits for them, and re-layouts  279 us (18%)
  other arithmetic  239 us (15%)
  starting transfers between devices  168 us (11%)
    ppermute x9, waiting for transfers between devices, per_device(): part = lax.ppermute(part, 'chan', [(d, d ^ mask) for d in range(ways)])  546 us
    all_to_all x3, starting transfers between devices, per_device(): lax.all_to_all(form_beams(turned, steering_matrix), 'chan', split_axis=2,...  137 us
    dot_general x3, matrix products, channelize(): jnp.einsum('oi,afi->oaf', forward, weighted, preferred_element_type=jnp.f...  96.3 us
    dot_general x3, matrix products, gram_block(): jnp.einsum('cif,cjf->cij', stacked, left_part, preferred_element_type=jnp...  86.9 us
    transpose x1, other arithmetic, synthesize(): return jnp.transpose(weighted.astype(jnp.bfloat16), (1, 0, 2, 3))  74.3 us
    another operation x1, other arithmetic  70.5 us
    dot_general x3, matrix products, form_beams(): jnp.einsum('goq,gqk->gok', steering_matrix, flattened_rows, preferred_ele...  64.4 us
    dot_general x3, matrix products, per_device(): jnp.einsum('oi,ibf->bfo', inverse_result, flattened_rows, preferred_eleme...  61.6 us
  transfers between devices with their start and end apart: 16, of which 6 were waited for; matrix products, arithmetic and copies ran while one was open for 40% of the time, Pallas kernels for 0%

profile of v1, /device:TPU:0, one launch (start us, length us, event | category | flops | bytes accessed | tf_op | source)
XLA Modules:
  0.0 1542.3 jit_solution(742002470681222398)
XLA Ops:
  2.0 4.9 collective-permute-start
  7.0 23.8 %bitcast_convert_fusion = (f32[128,256,128]{2,1,0:T(8,128)}, f32[128,256,128]{2,1,0:T(8,128)}, f32[128,256,128]{2,1,0:T(8,128)}) fusion(bf16[3,128,256,128]{3,2,1,0:T(8,128)(2,1)} %param.5), kind=kLoop, calls=%fused_computation.133 | loop fusion | flops 12582912 | bytes 75497472 | tf_op jit(solution)/shard_map/convert_element_type | solution.py:66
  32.1 32.5 %multiply_convert_fusion.4 = bf16[128,128,256]{2,0,1:T(8,128)(2,1)} fusion(f32[128]{0:T(128)S(1)} %convert_element_type.152, f32[128,3,128]{2,1,0:T(4,128)S(1)} %copy.73, f32[128,256,128]{2,1,0:T(8,128)} %get-tuple-element.12, f32[128]{0:T(128)S(1)} %get-tuple-element.45, f32[128]{0:T(128)S(1)} %get-tuple-element.46, f32[128]{0:T(128)S(1)} %get-tuple-element.47, ...), kind=kOutput, calls=%fused_computation.122 | convolution fusion | flops 1128595456 | bytes 25366272 | tf_op jit(solution)/shard_map/oi,afi->oaf/dot_general | solution.py:75
  64.6 13.2 reshape.193
  77.8 9.4 constant_dynamic-slice_fusion.4
  99.2 70.5 %fusion.102 = (bf16[16,512,512]{2,1,0:T(8,128)(2,1)}, bf16[16,512,512]{2,1,0:T(8,128)(2,1)}, bf16[16,512,512]{2,1,0:T(8,128)(2,1)}) fusion(s32[512,512]{1,0:T(8,128)S(1)} %copy.83, s32[16]{0:T(128)S(1)} %copy-done.18), kind=kLoop, calls=%fused_computation.143 | loop fusion | flops 75497472 | bytes 26214464 | tf_op jit(solution)/shard_map/convert.11
  169.6 4.3 broadcast.272.clone.1
  176.4 9.8 collective-permute-done.4
  186.2 3.2 constant_dynamic-update-slice_fusion.5
  189.4 46.5 %collective-permute-done.5 = bf16[16,2,128,256]{3,2,0,1:T(8,128)(2,1)} collective-permute-done((bf16[16,2,128,256]{3,2,0,1:T(8,128)(2,1)}, bf16[16,2,128,256]{3,2,0,1:T(8,128)(2,1)}, u32[]{:S(2)}, u32[]{:S(2)}) %collective-permute-start.5) | collective-permute-done | bytes 2097184 | tf_op jit(solution)/shard_map/ppermute | solution.py:151
  235.9 3.1 constant_dynamic-update-slice_fusion.4
  239.1 3.2 constant_dynamic-update-slice_fusion.3
  242.2 7.5 copy.89
  249.8 21.2 %multiply_convert_fusion.1 = bf16[16,1024,256]{2,1,0:T(8,128)(2,1)} fusion(bf16[16,1024,256]{2,1,0:T(8,128)(2,1)} %bitcast.161, bf16[16,512,512]{2,1,0:T(8,128)(2,1)} %get-tuple-element.33, bf16[16,512,512]{2,1,0:T(8,128)(2,1)} %get-tuple-element.32, bf16[16,512,512]{2,1,0:T(8,128)(2,1)} %get-tuple-element.31), kind=kOutput, calls=%fused_computation.117 | convolution fusion | flops 8732540928 | bytes 41943040 | tf_op jit(solution)/shard_map/goq,gqk->gok/dot_general | solution.py:90
  271.0 16.4 %copy.90 = bf16[16,2,512,256]{3,1,0,2:T(2,128)(2,1)} copy(bf16[16,2,512,256]{3,2,1,0:T(8,128)(2,1)} %bitcast.162) | data formatting | bytes 16777216 | tf_op jit(solution)/shard_map/reshape | solution.py:94
  287.4 43.3 %all-to-all-start.1 = ((bf16[16,2,512,256]{3,1,0,2:T(2,128)(2,1)}), bf16[16,2,512,256]{3,1,0,2:T(2,128)(2,1)}, u32[]{:S(2)}, u32[]{:S(2)}) async-start(bf16[16,2,512,256]{3,1,0,2:T(2,128)(2,1)} %copy.90), calls=%async_computation.1 | async-start | bytes 16777216 | tf_op jit(solution)/shard_map/all_to_all | solution.py:156
  330.9 31.9 %multiply_convert_fusion.5 = bf16[128,128,256]{2,0,1:T(8,128)(2,1)} fusion(f32[128]{0:T(128)S(1)} %copy-done.29, f32[128,3,128]{2,1,0:T(4,128)S(1)} %copy.68, f32[128,256,128]{2,1,0:T(8,128)} %get-tuple-element.11, f32[128]{0:T(128)S(1)} %copy-done.22, f32[128]{0:T(128)S(1)} %copy-done.24, f32[128]{0:T(128)S(1)} %copy-done.26, f32[128]{0:T(128)S(1)} %copy-done.20, ...), kind=kOutput, calls=%fused_computation.123 | convolution fusion | flops 1128595456 | bytes 25366272 | tf_op jit(solution)/shard_map/oi,afi->oaf/dot_general | solution.py:75
  362.7 13.1 reshape.192
  375.8 9.4 constant_dynamic-slice_fusion.8
  386.4 3.3 collective-permute-start.1
  394.9 4.3 broadcast.272.clone
  401.8 110.0 %collective-permute-done.1 = bf16[16,2,128,256]{3,2,0,1:T(8,128)(2,1)S(1)} collective-permute-done((bf16[16,2,128,256]{3,2,0,1:T(8,128)(2,1)S(1)}, bf16[16,2,128,256]{3,2,0,1:T(8,128)(2,1)S(1)}, u32[]{:S(2)}, u32[]{:S(2)}) %collective-permute-start.1) | collective-permute-done | bytes 2097184 | tf_op jit(solution)/shard_map/ppermute | solution.py:151
  513.2 134.9 %collective-permute-done.2 = bf16[16,2,128,256]{3,2,0,1:T(8,128)(2,1)S(1)} collective-permute-done((bf16[16,2,128,256]{3,2,0,1:T(8,128)(2,1)S(1)}, bf16[16,2,128,256]{3,2,0,1:T(8,128)(2,1)S(1)}, u32[]{:S(2)}, u32[]{:S(2)}) %collective-permute-start.2) | collective-permute-done | bytes 2097184 | tf_op jit(solution)/shard_map/ppermute | solution.py:151
  651.0 7.5 copy.84
  658.5 21.8 %multiply_convert_fusion.2 = bf16[16,1024,256]{2,1,0:T(8,128)(2,1)} fusion(bf16[16,1024,256]{2,1,0:T(8,128)(2,1)} %bitcast.164, bf16[16,512,512]{2,1,0:T(8,128)(2,1)} %get-tuple-element.33, bf16[16,512,512]{2,1,0:T(8,128)(2,1)} %get-tuple-element.32, bf16[16,512,512]{2,1,0:T(8,128)(2,1)} %get-tuple-element.31), kind=kOutput, calls=%fused_computation.118 | convolution fusion | flops 8732540928 | bytes 41943040 | tf_op jit(solution)/shard_map/goq,gqk->gok/dot_general | solution.py:90
  680.3 16.4 %copy.85 = bf16[16,2,512,256]{3,1,0,2:T(2,128)(2,1)} copy(bf16[16,2,512,256]{3,2,1,0:T(8,128)(2,1)} %bitcast.163) | data formatting | bytes 16777216 | tf_op jit(solution)/shard_map/reshape | solution.py:94
  696.8 46.2 %all-to-all-start = ((bf16[16,2,512,256]{3,1,0,2:T(2,128)(2,1)}), bf16[16,2,512,256]{3,1,0,2:T(2,128)(2,1)}, u32[]{:S(2)}, u32[]{:S(2)}) async-start(bf16[16,2,512,256]{3,1,0,2:T(2,128)(2,1)} %copy.85), calls=%async_computation | async-start | bytes 16777216 | tf_op jit(solution)/shard_map/all_to_all | solution.py:156
  743.0 32.0 %multiply_convert_fusion.3 = bf16[128,128,256]{2,0,1:T(8,128)(2,1)} fusion(f32[128]{0:T(128)S(1)} %copy-done.29, f32[128,3,128]{2,1,0:T(4,128)S(1)} %copy.78, f32[128,256,128]{2,1,0:T(8,128)} %get-tuple-element.10, f32[128]{0:T(128)S(1)} %copy-done.22, f32[128]{0:T(128)S(1)} %copy-done.24, f32[128]{0:T(128)S(1)} %copy-done.26, f32[128]{0:T(128)S(1)} %copy-done.20, ...), kind=kOutput, calls=%fused_computation.121 | convolution fusion | flops 1128595456 | bytes 25366272 | tf_op jit(solution)/shard_map/oi,afi->oaf/dot_general | solution.py:75
  774.9 13.1 reshape.194
  788.0 9.4 constant_dynamic-slice_fusion
  798.6 3.5 collective-permute-start.7
  807.7 4.3 broadcast.272.clone.2
  814.6 109.5 %collective-permute-done.7 = bf16[16,2,128,256]{3,2,0,1:T(8,128)(2,1)S(1)} collective-permute-done((bf16[16,2,128,256]{3,2,0,1:T(8,128)(2,1)S(1)}, bf16[16,2,128,256]{3,2,0,1:T(8,128)(2,1)S(1)}, u32[]{:S(2)}, u32[]{:S(2)}) %collective-permute-start.7) | collective-permute-done | bytes 2097184 | tf_op jit(solution)/shard_map/ppermute | solution.py:151
  925.5 135.6 %collective-permute-done.8 = bf16[16,2,128,256]{3,2,0,1:T(8,128)(2,1)S(1)} collective-permute-done((bf16[16,2,128,256]{3,2,0,1:T(8,128)(2,1)S(1)}, bf16[16,2,128,256]{3,2,0,1:T(8,128)(2,1)S(1)}, u32[]{:S(2)}, u32[]{:S(2)}) %collective-permute-start.8) | collective-permute-done | bytes 2097184 | tf_op jit(solution)/shard_map/ppermute | solution.py:151
  1064.0 7.5 copy.94
  1071.5 21.4 %multiply_convert_fusion = bf16[16,1024,256]{2,1,0:T(8,128)(2,1)} fusion(bf16[16,1024,256]{2,1,0:T(8,128)(2,1)} %bitcast.160, bf16[16,512,512]{2,1,0:T(8,128)(2,1)} %get-tuple-element.33, bf16[16,512,512]{2,1,0:T(8,128)(2,1)} %get-tuple-element.32, bf16[16,512,512]{2,1,0:T(8,128)(2,1)} %get-tuple-element.31), kind=kOutput, calls=%fused_computation.116 | convolution fusion | flops 8732540928 | bytes 41943040 | tf_op jit(solution)/shard_map/goq,gqk->gok/dot_general | solution.py:90
  1092.9 16.4 %copy.95 = bf16[16,2,512,256]{3,1,0,2:T(2,128)(2,1)} copy(bf16[16,2,512,256]{3,2,1,0:T(8,128)(2,1)} %bitcast.159) | data formatting | bytes 16777216 | tf_op jit(solution)/shard_map/reshape | solution.py:94
  1109.3 4.6 fusion.175
  1113.9 4.5 fusion.174
  1118.3 5.9 slice_bitcast_fusion.3
  1124.2 5.9 slice_bitcast_fusion.5
  1130.1 5.9 slice_bitcast_fusion.1
  1136.0 47.2 %all-to-all-start.2 = ((bf16[16,2,512,256]{3,1,0,2:T(2,128)(2,1)}), bf16[16,2,512,256]{3,1,0,2:T(2,128)(2,1)}, u32[]{:S(2)}, u32[]{:S(2)}) async-start(bf16[16,2,512,256]{3,1,0,2:T(2,128)(2,1)} %copy.95), calls=%async_computation.2 | async-start | bytes 16777216 | tf_op jit(solution)/shard_map/all_to_all | solution.py:156
  1183.2 4.5 fusion.173
  1187.7 23.4 %fusion.60 = f32[16,1024,512]{2,1,0:T(8,128)} fusion(bf16[16,512,256]{2,1,0:T(8,128)(2,1)} %fusion.173, bf16[16,512,256]{2,1,0:T(8,128)(2,1)} %get-tuple-element.26, bf16[16,512,256]{2,1,0:T(8,128)(2,1)} %get-tuple-element.25), kind=kOutput, calls=%fused_computation.92 | convolution fusion | flops 8673820672 | bytes 46137344 | tf_op jit(solution)/shard_map/cif,cjf->cij/dot_general | solution.py:84
  1211.1 22.7 %fusion.68 = f32[16,1024,512]{2,1,0:T(8,128)} fusion(bf16[16,512,256]{2,1,0:T(8,128)(2,1)S(1)} %copy-done.2, bf16[16,512,256]{2,1,0:T(8,128)(2,1)} %get-tuple-element.20, bf16[16,512,256]{2,1,0:T(8,128)(2,1)} %get-tuple-element.19), kind=kOutput, calls=%fused_computation.100 | convolution fusion | flops 8673820672 | bytes 46137344 | tf_op jit(solution)/shard_map/cif,cjf->cij/dot_general | solution.py:84
  1233.8 40.8 %add_multiply_fusion = f32[16,1024,512]{2,1,0:T(8,128)} fusion(f32[16,1024,512]{2,1,0:T(8,128)} %fusion.60, f32[16,1024,512]{2,1,0:T(8,128)} %fusion.68, bf16[16,512,256]{2,1,0:T(8,128)(2,1)} %fusion.175, bf16[16,512,256]{2,1,0:T(8,128)(2,1)} %get-tuple-element.14, bf16[16,512,256]{2,1,0:T(8,128)(2,1)} %get-tuple-element.13), kind=kOutput, calls=%fused_computation.1 | convolution fusion | flops 8698986496 | bytes 113246208 | tf_op jit(solution)/shard_map/cif,cjf->cij/dot_general | solution.py:84
  1274.6 11.6 copy.91
  1286.2 7.8 copy.92
  1294.0 19.6 %fusion.112 = bf16[128,256,128]{2,1,0:T(8,128)(2,1)S(1)} fusion(bf16[128,128,256]{2,1,0:T(8,128)(2,1)} %bitcast.155, s32[128]{0:T(128)S(1)} %copy-done.11, s32[128]{0:T(128)S(1)} %copy-done.9, pred[128]{0:T(512)(128)(4,1)S(1)} %copy-done.5, pred[128]{0:T(512)(128)(4,1)S(1)} %copy-done.7), kind=kOutput, calls=%fused_computation.148 | convolution fusion | flops 1078263808 | bytes 16778496 | tf_op jit(solution)/shard_map/oi,ibf->bfo/dot_general | solution.py:161
  1313.6 3.3 copy-done
  1316.9 5.2 collective-permute-start.11
  1322.2 11.6 copy.86
  1333.7 7.8 copy.87
  1341.5 19.4 %fusion.109 = bf16[128,256,128]{2,1,0:T(8,128)(2,1)S(1)} fusion(bf16[128,128,256]{2,1,0:T(8,128)(2,1)} %bitcast.157, s32[128]{0:T(128)S(1)} %copy-done.11, s32[128]{0:T(128)S(1)} %copy-done.9, pred[128]{0:T(512)(128)(4,1)S(1)} %copy-done.5, pred[128]{0:T(512)(128)(4,1)S(1)} %copy-done.7), kind=kOutput, calls=%fused_computation.147 | convolution fusion | flops 1078263808 | bytes 16778496 | tf_op jit(solution)/shard_map/oi,ibf->bfo/dot_general | solution.py:161
  1360.9 3.3 copy-done.1
  1366.6 11.8 convert_bitcast_fusion.2
  1378.4 11.4 copy.96
  1389.8 7.8 copy.97
  1397.6 22.6 %fusion.115 = bf16[128,256,128]{2,1,0:T(8,128)(2,1)} fusion(bf16[128,128,256]{2,1,0:T(8,128)(2,1)} %bitcast.153, s32[128]{0:T(128)S(1)} %copy-done.11, s32[128]{0:T(128)S(1)} %copy-done.9, pred[128]{0:T(512)(128)(4,1)S(1)} %copy-done.5, pred[128]{0:T(512)(128)(4,1)S(1)} %copy-done.7), kind=kOutput, calls=%fused_computation.149 | convolution fusion | flops 1078263808 | bytes 16778496 | tf_op jit(solution)/shard_map/oi,ibf->bfo/dot_general | solution.py:161
  1420.2 11.6 convert_bitcast_fusion
  1435.3 11.5 convert_bitcast_fusion.1
  1447.0 74.3 %fusion.108 = (bf16[1,128,256,128]{3,2,1,0:T(8,128)(2,1)}, bf16[1,128,256,128]{3,2,1,0:T(8,128)(2,1)}, bf16[1,128,256,128]{3,2,1,0:T(8,128)(2,1)}) fusion(f32[128,1,256,128]{3,2,0,1:T(8,128)} %convert_bitcast_fusion.2, f32[128,1,3,128]{3,2,0,1:T(4,128)S(1)} %convert_element_type.172, f32[128]{0:T(128)S(1)} %copy-done.15, f32[128]{0:T(128)S(1)} %copy-done.16, ...), kind=kLoop, calls=%fused_computation.146 | loop fusion | flops 150994944 | bytes 101255168 | tf_op jit(solution)/shard_map/transpose | solution.py:117
  1521.3 20.7 %pad_maximum_fusion = bf16[3,128,256,128]{3,2,1,0:T(8,128)(2,1)} fusion(bf16[1,128,256,128]{3,2,1,0:T(8,128)(2,1)} %get-tuple-element.39, bf16[1,128,256,128]{3,2,1,0:T(8,128)(2,1)} %get-tuple-element.38, bf16[1,128,256,128]{3,2,1,0:T(8,128)(2,1)} %get-tuple-element.37), kind=kLoop, calls=%fused_computation.5 | loop fusion | flops 25165824 | bytes 50331648 | tf_op jit(solution)/shard_map/concatenate | solution.py:167
  (116 shorter events, 50.2 us)
Async XLA Ops:
  2.0 29.9 %collective-permute-start = (bf16[3,128,3,128]{3,1,2,0:T(8,128)(2,1)S(1)}, bf16[3,128,3,128]{3,1,2,0:T(8,128)(2,1)S(1)}, u32[]{:S(2)}, u32[]{:S(2)}) collective-permute-start(bf16[3,128,3,128]{3,1,2,0:T(8,128)(2,1)S(1)} %copy.100), channel_id=1, source_target_pairs={{0,1},{1,8},{8,9},{9,16},{16,17},{17,24},{24,25},{2,3},{3,10},{10,... | collective-permute-start | bytes 884744 | tf_op jit(solution)/shard_map/ppermute | solution.py:17
  7.0 736.0 %copy-start.4 = (pred[128]{0:T(512)(128)(4,1)}, pred[128]{0:T(512)(128)(4,1)S(1)}, u32[]{:S(2)}) copy-start(pred[128]{0:T(512)(128)(4,1)S(1)} %get-tuple-element.50) | copy-start | bytes 388
  7.0 736.0 %copy-start.6 = (pred[128]{0:T(512)(128)(4,1)}, pred[128]{0:T(512)(128)(4,1)S(1)}, u32[]{:S(2)}) copy-start(pred[128]{0:T(512)(128)(4,1)S(1)} %get-tuple-element.51) | copy-start | bytes 388
  7.0 736.0 %copy-start.8 = (s32[128]{0:T(128)}, s32[128]{0:T(128)S(1)}, u32[]{:S(2)}) copy-start(s32[128]{0:T(128)S(1)} %get-tuple-element.48) | copy-start | bytes 1540
  7.0 736.0 %copy-start.10 = (s32[128]{0:T(128)}, s32[128]{0:T(128)S(1)}, u32[]{:S(2)}) copy-start(s32[128]{0:T(128)S(1)} %get-tuple-element.49) | copy-start | bytes 1540
  7.0 23.8 %copy-start.27 = (s32[128]{0:T(128)S(1)}, s32[128]{0:T(128)}, u32[]{:S(2)}) copy-start(s32[128]{0:T(128)} %param.6) | copy-start | bytes 1540
  7.0 23.8 %copy-start.12 = (f32[4,64]{1,0:T(4,128)S(1)}, f32[4,64]{1,0:T(4,128)}, u32[]{:S(2)}) copy-start(f32[4,64]{1,0:T(4,128)} %param.8) | copy-start | bytes 3076
  7.0 23.9 %copy-start.3 = (s32[512,512]{1,0:T(8,128)S(1)}, s32[512,512]{1,0:T(8,128)}, u32[]{:S(2)}) copy-start(s32[512,512]{1,0:T(8,128)} %param.7) | copy-start | bytes 3145732
  30.8 33.7 %copy-start.28 = (f32[128]{0:T(128)}, f32[128]{0:T(128)S(1)}, u32[]{:S(2)}) copy-start(f32[128]{0:T(128)S(1)} %convert_element_type.152) | copy-start | bytes 1540
  31.9 32.7 %copy-start.19 = (f32[128]{0:T(128)}, f32[128]{0:T(128)S(1)}, u32[]{:S(2)}) copy-start(f32[128]{0:T(128)S(1)} %get-tuple-element.44) | copy-start | bytes 1540
  31.9 32.7 %copy-start.21 = (f32[128]{0:T(128)}, f32[128]{0:T(128)S(1)}, u32[]{:S(2)}) copy-start(f32[128]{0:T(128)S(1)} %get-tuple-element.45) | copy-start | bytes 1540
  31.9 32.7 %copy-start.23 = (f32[128]{0:T(128)}, f32[128]{0:T(128)S(1)}, u32[]{:S(2)}) copy-start(f32[128]{0:T(128)S(1)} %get-tuple-element.46) | copy-start | bytes 1540
  31.9 32.7 %copy-start.25 = (f32[128]{0:T(128)}, f32[128]{0:T(128)S(1)}, u32[]{:S(2)}) copy-start(f32[128]{0:T(128)S(1)} %get-tuple-element.47) | copy-start | bytes 1540
  77.8 21.4 %copy-start.18 = (s32[16]{0:T(128)S(1)}, s32[16]{0:T(128)}, u32[]{:S(2)}) copy-start(s32[16]{0:T(128)} %multiply_add_fusion) | copy-start | bytes 196
  94.8 91.4 %collective-permute-start.4 = (bf16[16,2,128,256]{3,2,0,1:T(8,128)(2,1)}, bf16[16,2,128,256]{3,2,0,1:T(8,128)(2,1)}, u32[]{:S(2)}, u32[]{:S(2)}) collective-permute-start(bf16[16,2,128,256]{3,2,0,1:T(8,128)(2,1)} %copy.106), channel_id=1, source_target_pairs={{0,2},{2,0},{4,6},{6,4},{1,3},{3,1},{5,7},{7,5},{8,10},{10,8},{12,... | collective-permute-start | bytes 6291464 | tf_op jit(solution)/shard_map/ppermute | solution.py:151
  96.4 139.6 %collective-permute-start.5 = (bf16[16,2,128,256]{3,2,0,1:T(8,128)(2,1)}, bf16[16,2,128,256]{3,2,0,1:T(8,128)(2,1)}, u32[]{:S(2)}, u32[]{:S(2)}) collective-permute-start(bf16[16,2,128,256]{3,2,0,1:T(8,128)(2,1)} %copy.107), channel_id=1, source_target_pairs={{0,4},{2,6},{4,0},{6,2},{1,5},{3,7},{5,1},{7,3},{8,12},{10,14},{12... | collective-permute-start | bytes 6291464 | tf_op jit(solution)/shard_map/ppermute | solution.py:151
  98.9 140.2 %collective-permute-start.6 = (bf16[16,2,128,256]{3,2,0,1:T(8,128)(2,1)}, bf16[16,2,128,256]{3,2,0,1:T(8,128)(2,1)}, u32[]{:S(2)}, u32[]{:S(2)}) collective-permute-start(bf16[16,2,128,256]{3,2,0,1:T(8,128)(2,1)} %copy.108), channel_id=1, source_target_pairs={{0,6},{2,4},{4,2},{6,0},{1,7},{3,5},{5,3},{7,1},{8,14},{10,12},{12... | collective-permute-start | bytes 6291464 | tf_op jit(solution)/shard_map/ppermute | solution.py:151
  271.0 59.8 %copy-start.20 = (f32[128]{0:T(128)S(1)}, f32[128]{0:T(128)}, u32[]{:S(2)}) copy-start(f32[128]{0:T(128)} %copy-done.19) | copy-start | bytes 1540
  271.0 59.9 %copy-start.22 = (f32[128]{0:T(128)S(1)}, f32[128]{0:T(128)}, u32[]{:S(2)}) copy-start(f32[128]{0:T(128)} %copy-done.21) | copy-start | bytes 1540
  271.0 59.9 %copy-start.24 = (f32[128]{0:T(128)S(1)}, f32[128]{0:T(128)}, u32[]{:S(2)}) copy-start(f32[128]{0:T(128)} %copy-done.23) | copy-start | bytes 1540
  271.0 59.9 %copy-start.26 = (f32[128]{0:T(128)S(1)}, f32[128]{0:T(128)}, u32[]{:S(2)}) copy-start(f32[128]{0:T(128)} %copy-done.25) | copy-start | bytes 1540
  271.0 59.9 %copy-start.29 = (f32[128]{0:T(128)S(1)}, f32[128]{0:T(128)}, u32[]{:S(2)}) copy-start(f32[128]{0:T(128)} %copy-done.28) | copy-start | bytes 1540
  287.4 409.3 %all-to-all-start.1 = ((bf16[16,2,512,256]{3,1,0,2:T(2,128)(2,1)}), bf16[16,2,512,256]{3,1,0,2:T(2,128)(2,1)}, u32[]{:S(2)}, u32[]{:S(2)}) async-start(bf16[16,2,512,256]{3,1,0,2:T(2,128)(2,1)} %copy.90), calls=%async_computation.1 | async-start | bytes 16777216 | tf_op jit(solution)/shard_map/all_to_all | solution.py:156
  386.4 125.3 %collective-permute-start.1 = (bf16[16,2,128,256]{3,2,0,1:T(8,128)(2,1)S(1)}, bf16[16,2,128,256]{3,2,0,1:T(8,128)(2,1)S(1)}, u32[]{:S(2)}, u32[]{:S(2)}) collective-permute-start(bf16[16,2,128,256]{3,2,0,1:T(8,128)(2,1)S(1)} %copy.102), channel_id=1, source_target_pairs={{0,2},{2,0},{4,6},{6,4},{1,3},{3,1},{5,7},{7,5},{8,10},{10,8},{12,... | collective-permute-start | bytes 6291464 | tf_op jit(solution)/shard_map/ppermute | solution.py:151
  391.0 257.2 %collective-permute-start.2 = (bf16[16,2,128,256]{3,2,0,1:T(8,128)(2,1)S(1)}, bf16[16,2,128,256]{3,2,0,1:T(8,128)(2,1)S(1)}, u32[]{:S(2)}, u32[]{:S(2)}) collective-permute-start(bf16[16,2,128,256]{3,2,0,1:T(8,128)(2,1)S(1)} %copy.103), channel_id=1, source_target_pairs={{0,4},{2,6},{4,0},{6,2},{1,5},{3,7},{5,1},{7,3},{8,12},{10,14},{12... | collective-permute-start | bytes 6291464 | tf_op jit(solution)/shard_map/ppermute | solution.py:151
  393.3 256.3 %collective-permute-start.3 = (bf16[16,2,128,256]{3,2,0,1:T(8,128)(2,1)S(1)}, bf16[16,2,128,256]{3,2,0,1:T(8,128)(2,1)S(1)}, u32[]{:S(2)}, u32[]{:S(2)}) collective-permute-start(bf16[16,2,128,256]{3,2,0,1:T(8,128)(2,1)S(1)} %copy.104), channel_id=1, source_target_pairs={{0,6},{2,4},{4,2},{6,0},{1,7},{3,5},{5,3},{7,1},{8,14},{10,12},{12... | collective-permute-start | bytes 6291464 | tf_op jit(solution)/shard_map/ppermute | solution.py:151
  696.8 439.3 %all-to-all-start = ((bf16[16,2,512,256]{3,1,0,2:T(2,128)(2,1)}), bf16[16,2,512,256]{3,1,0,2:T(2,128)(2,1)}, u32[]{:S(2)}, u32[]{:S(2)}) async-start(bf16[16,2,512,256]{3,1,0,2:T(2,128)(2,1)} %copy.85), calls=%async_computation | async-start | bytes 16777216 | tf_op jit(solution)/shard_map/all_to_all | solution.py:156
  788.0 19.1 %copy-start.13 = (f32[4,64]{1,0:T(4,128)S(1)}, f32[4,64]{1,0:T(4,128)}, u32[]{:S(2)}) copy-start(f32[4,64]{1,0:T(4,128)} %param.9) | copy-start | bytes 3076
  798.6 125.4 %collective-permute-start.7 = (bf16[16,2,128,256]{3,2,0,1:T(8,128)(2,1)S(1)}, bf16[16,2,128,256]{3,2,0,1:T(8,128)(2,1)S(1)}, u32[]{:S(2)}, u32[]{:S(2)}) collective-permute-start(bf16[16,2,128,256]{3,2,0,1:T(8,128)(2,1)S(1)} %copy.110), channel_id=1, source_target_pairs={{0,2},{2,0},{4,6},{6,4},{1,3},{3,1},{5,7},{7,5},{8,10},{10,8},{12,... | collective-permute-start | bytes 6291464 | tf_op jit(solution)/shard_map/ppermute | solution.py:151
  803.3 257.7 %collective-permute-start.8 = (bf16[16,2,128,256]{3,2,0,1:T(8,128)(2,1)S(1)}, bf16[16,2,128,256]{3,2,0,1:T(8,128)(2,1)S(1)}, u32[]{:S(2)}, u32[]{:S(2)}) collective-permute-start(bf16[16,2,128,256]{3,2,0,1:T(8,128)(2,1)S(1)} %copy.111), channel_id=1, source_target_pairs={{0,4},{2,6},{4,0},{6,2},{1,5},{3,7},{5,1},{7,3},{8,12},{10,14},{12... | collective-permute-start | bytes 6291464 | tf_op jit(solution)/shard_map/ppermute | solution.py:151
  805.5 257.0 %collective-permute-start.9 = (bf16[16,2,128,256]{3,2,0,1:T(8,128)(2,1)S(1)}, bf16[16,2,128,256]{3,2,0,1:T(8,128)(2,1)S(1)}, u32[]{:S(2)}, u32[]{:S(2)}) collective-permute-start(bf16[16,2,128,256]{3,2,0,1:T(8,128)(2,1)S(1)} %copy.112), channel_id=1, source_target_pairs={{0,6},{2,4},{4,2},{6,0},{1,7},{3,5},{5,3},{7,1},{8,14},{10,12},{12... | collective-permute-start | bytes 6291464 | tf_op jit(solution)/shard_map/ppermute | solution.py:151
  1136.0 242.4 %all-to-all-start.2 = ((bf16[16,2,512,256]{3,1,0,2:T(2,128)(2,1)}), bf16[16,2,512,256]{3,1,0,2:T(2,128)(2,1)}, u32[]{:S(2)}, u32[]{:S(2)}) async-start(bf16[16,2,512,256]{3,1,0,2:T(2,128)(2,1)} %copy.95), calls=%async_computation.2 | async-start | bytes 16777216 | tf_op jit(solution)/shard_map/all_to_all | solution.py:156
  1187.7 23.4 %copy-start.2 = (bf16[16,512,256]{2,1,0:T(8,128)(2,1)S(1)}, bf16[16,512,256]{2,1,0:T(8,128)(2,1)}, u32[]{:S(2)}) copy-start(bf16[16,512,256]{2,1,0:T(8,128)(2,1)} %fusion.174) | copy-start | bytes 12582916
  1274.6 19.4 %copy-start.5 = (pred[128]{0:T(512)(128)(4,1)S(1)}, pred[128]{0:T(512)(128)(4,1)}, u32[]{:S(2)}) copy-start(pred[128]{0:T(512)(128)(4,1)} %copy-done.4) | copy-start | bytes 388
  1274.6 19.4 %copy-start.7 = (pred[128]{0:T(512)(128)(4,1)S(1)}, pred[128]{0:T(512)(128)(4,1)}, u32[]{:S(2)}) copy-start(pred[128]{0:T(512)(128)(4,1)} %copy-done.6) | copy-start | bytes 388
  1274.6 19.4 %copy-start.9 = (s32[128]{0:T(128)S(1)}, s32[128]{0:T(128)}, u32[]{:S(2)}) copy-start(s32[128]{0:T(128)} %copy-done.8) | copy-start | bytes 1540
  1274.6 19.4 %copy-start.11 = (s32[128]{0:T(128)S(1)}, s32[128]{0:T(128)}, u32[]{:S(2)}) copy-start(s32[128]{0:T(128)} %copy-done.10) | copy-start | bytes 1540
  1313.6 3.3 copy-start
  1316.9 129.9 %collective-permute-start.11 = (bf16[128,1,3,128]{3,2,0,1:T(4,128)(2,1)S(1)}, bf16[128,1,3,128]{3,2,0,1:T(4,128)(2,1)S(1)}, u32[]{:S(2)}, u32[]{:S(2)}) collective-permute-start(bf16[128,1,3,128]{3,2,0,1:T(4,128)(2,1)S(1)} %slice.216), channel_id=1, source_target_pairs={{0,1},{1,8},{8,9},{9,16},{16,17},{17,24},{24,25},{2,3},{3,10},{10,... | collective-permute-start | bytes 294920 | tf_op jit(solution)/shard_map/ppermute | solution.py:17
  1360.9 3.3 copy-start.1
  1364.3 82.6 %collective-permute-start.10 = (bf16[128,1,3,128]{3,2,0,1:T(4,128)(2,1)S(1)}, bf16[128,1,3,128]{3,2,0,1:T(4,128)(2,1)S(1)}, u32[]{:S(2)}, u32[]{:S(2)}) collective-permute-start(bf16[128,1,3,128]{3,2,0,1:T(4,128)(2,1)S(1)} %slice.211), channel_id=1, source_target_pairs={{0,1},{1,8},{8,9},{9,16},{16,17},{17,24},{24,25},{2,3},{3,10},{10,... | collective-permute-start | bytes 294920 | tf_op jit(solution)/shard_map/ppermute | solution.py:17
  1431.9 15.1 copy-start.14
  1431.9 15.1 copy-start.15
  1431.9 15.1 copy-start.16
  1431.9 15.1 copy-start.17
  1432.9 14.0 collective-permute-start.12
